TPU v7x, 128 devices: a whole 4x4x4 slice. The times are simulated.
128 devices in a mesh: var: 16 (over x_hi, z, core), tp: 8 (over y, x_lo).
Axes of the slice: x: 4 (x_hi: 2, x_lo: 2; x = x_hi * 2 + x_lo), y: 4, z: 4, core: 2. Of those that a mesh axis runs over, the one named last changes fastest.
Arguments:
- hidden_in: bfloat16 [48, 384, 2048], P('var'), may hold values from -100 to 100
- run_table: int32 [48, 2], P('var'), may hold values 0 or 1
- qkv_weight: bfloat16 [2048, 3072], P('var', 'tp'), may hold values from -1 to 1
- out_weight: bfloat16 [2048, 2048], P('tp', 'var'), may hold values from -0.125 to 0.125
- gate_up_weight: bfloat16 [2048, 2, 8192], P('var', None, 'tp'), may hold values from -0.125 to 0.125
- down_weight: bfloat16 [8192, 2048], P('tp', 'var'), may hold values from -0.0625 to 0.0625
Outputs:
- layer_out: bfloat16 [48, 384, 2048], P('var')
All inputs are finite; a program needn't handle non-finite values. No bound on the sum of `run_table` on one device may be relied on, other than what follows from the above.
Results may differ from a plain program's by a relative error of at most 0.0075.
Values may be sent and summed in bfloat16 or wider, within the bound.
No kernel may reach another device: no remote copies, remote signals or barrier semaphores. Data moves between devices by JAX's collectives and lax.ppermute only.
A program may use at most 128 MiB of HBM per device.

v0:
```python
import jax
import jax.numpy as jnp
from jax import lax
from jax.sharding import PartitionSpec as P

QUERY_HEADS = 32
KEY_VALUE_HEADS = 8
HEAD_SIZE = 64


def rms_norm(tensor):
    widened = tensor.astype(jnp.float32)
    scaled = widened * lax.rsqrt(jnp.mean(widened * widened, axis=-1, keepdims=True) + 1e-05)
    return scaled.astype(jnp.bfloat16)


def rotary_embedding(tensor, token_positions):
    half_width = tensor.shape[-1] // 2
    exponent = jnp.arange(half_width, dtype=jnp.float32) * (2.0 / tensor.shape[-1])
    frequency = jnp.power(jnp.float32(500000.0), -exponent)
    angles = token_positions[:, None, None] * frequency[None, None, :]
    cosine = jnp.cos(angles)
    sine_part = jnp.sin(angles)
    first_half = tensor[..., :half_width]
    second_half = tensor[..., half_width:]
    return jnp.concatenate(
        [
            first_half * cosine - second_half * sine_part,
            second_half * cosine + first_half * sine_part,
        ],
        axis=-1,
    )


def attend(query_rows, keys_bfloat, values_bfloat, score_scale):
    scores = (
        jnp.einsum("bqkgd,bpkd->bkgqp", query_rows, keys_bfloat, preferred_element_type=jnp.float32)
        * score_scale
    )
    length = scores.shape[-1]
    causal = jnp.arange(length)[:, None] >= jnp.arange(length)[None, :]
    scores = jnp.where(causal, scores, jnp.float32(-1e30))
    row_max = jnp.max(scores, axis=-1, keepdims=True)
    exped = jnp.exp(scores - row_max)
    weights_bf = (exped / jnp.sum(exped, axis=-1, keepdims=True)).astype(jnp.bfloat16)
    head_outputs = jnp.einsum(
        "bkgqp,bpkd->bqkgd", weights_bf, values_bfloat, preferred_element_type=jnp.float32
    )
    return head_outputs.astype(jnp.bfloat16)


def shards(hidden_in, run_table, qkv_weight, out_weight, gate_up_weight, down_weight):
    tensor_parallel_count = lax.axis_size("tp")
    seq_count, full_len, model_width = hidden_in.shape
    row_count = seq_count * full_len
    query_slice = QUERY_HEADS // tensor_parallel_count
    key_value_slice = KEY_VALUE_HEADS // tensor_parallel_count
    group_width = QUERY_HEADS // KEY_VALUE_HEADS
    switches = run_table.astype(jnp.float32)
    flat_input = rms_norm(hidden_in).reshape(row_count, model_width)
    columns = flat_input
    projected_rows = jnp.dot(
        columns,
        lax.all_gather(qkv_weight, "var", axis=0, tiled=True),
        preferred_element_type=jnp.float32,
    )
    projected_rows = projected_rows.reshape(
        seq_count, full_len, query_slice + 2 * key_value_slice, HEAD_SIZE
    )
    token_positions = jnp.arange(full_len, dtype=jnp.float32)
    query_rows = rotary_embedding(projected_rows[:, :, :query_slice], token_positions).astype(
        jnp.bfloat16
    )
    query_rows = query_rows.reshape(seq_count, full_len, key_value_slice, group_width, HEAD_SIZE)
    keys_bfloat = rotary_embedding(
        projected_rows[:, :, query_slice : query_slice + key_value_slice], token_positions
    ).astype(jnp.bfloat16)
    values_bfloat = projected_rows[:, :, query_slice + key_value_slice :].astype(jnp.bfloat16)
    score_scale = HEAD_SIZE ** (-0.5)
    head_outputs = attend(query_rows, keys_bfloat, values_bfloat, score_scale)
    head_rows = head_outputs.reshape(row_count, query_slice * HEAD_SIZE)
    attn_terms = jnp.dot(
        head_rows,
        lax.all_gather(out_weight, "var", axis=1, tiled=True),
        preferred_element_type=jnp.float32,
    )
    attn_terms = attn_terms.reshape(seq_count, full_len, model_width)
    attn_switch = switches[:, 0][:, None, None]
    attention = lax.psum(attn_terms.astype(jnp.bfloat16), "tp").astype(jnp.float32)
    whole_after = (hidden_in.astype(jnp.float32) + attn_switch * attention).astype(jnp.bfloat16)
    mlp_input = rms_norm(whole_after)
    flat_mlp = mlp_input.reshape(row_count, model_width)
    ff_local = gate_up_weight.shape[2]
    block_piece = lax.all_gather(gate_up_weight, "var", axis=0, tiled=True)
    columns = flat_mlp
    flat_piece = block_piece.reshape(block_piece.shape[0], 2 * ff_local)
    gate_and_up = jnp.dot(columns, flat_piece, preferred_element_type=jnp.float32)
    hidden = (jax.nn.silu(gate_and_up[:, :ff_local]) * gate_and_up[:, ff_local:]).astype(
        jnp.bfloat16
    )
    mlp_terms = jnp.dot(
        hidden,
        lax.all_gather(down_weight, "var", axis=1, tiled=True),
        preferred_element_type=jnp.float32,
    )
    mlp_terms = mlp_terms.reshape(seq_count, full_len, model_width)
    mlp = lax.psum(mlp_terms.astype(jnp.bfloat16), "tp").astype(jnp.float32)
    mlp_switch = switches[:, 1][:, None, None]
    return (whole_after.astype(jnp.float32) + mlp_switch * mlp).astype(jnp.bfloat16)


def solution(mesh):
    return jax.shard_map(
        shards,
        mesh=mesh,
        in_specs=(
            P("var", None, None),
            P("var", None),
            P("var", "tp"),
            P("tp", "var"),
            P("var", None, "tp"),
            P("tp", "var"),
        ),
        out_specs=P("var", None, None),
        check_vma=False,
    )
```

profile of v0, /device:TPU:1, one launch (start us, length us, event | category | flops | bytes accessed | tf_op | source)
XLA Modules:
  0.0 667.6 jit_solution(8248139366592149826)
XLA Ops:
  6.5 0.7 all-gather.5.cloned.1.call-update
  7.3 0.7 all-gather.7.cloned.1.call-update
  8.1 3.3 fusion
  11.7 47.8 %all-gather.5.cloned.1.call-done = bf16[2048,384]{1,0:T(8,128)(2,1)} async-done(((bf16[128,384]{1,0:T(8,128)(2,1)}), bf16[2048,384]{1,0:T(8,128)(2,1)}) %all-gather.5.cloned.1.call-update) | async-done | bytes 1572880 | tf_op jit(solution)/shard_map/all_gather | solution.py:64
  59.5 1.7 copy.14
  61.2 4.6 fusion.9
  66.1 1.2 fusion.7
  67.3 1.5 fusion.6
  68.8 2.1 fusion.17
  70.9 32.4 %all-gather.7.cloned.1.call-done = bf16[256,2048]{1,0:T(8,128)(2,1)} async-done(((bf16[256,128]{1,0:T(8,128)(2,1)}), bf16[256,2048]{1,0:T(8,128)(2,1)}) %all-gather.7.cloned.1.call-update) | async-done | bytes 1048592 | tf_op jit(solution)/shard_map/all_gather | solution.py:84
  103.3 4.8 convolution_convert_fusion.1
  108.2 0.5 all-gather.9.cloned.1.call-update
  108.8 0.5 all-gather.11.cloned.1.call-update
  109.6 200.1 %all-reduce.3.cloned.1.call-done = bf16[3,384,2048]{2,1,0:T(8,128)(2,1)} async-done(((bf16[3,384,2048]{2,1,0:T(8,128)(2,1)}), bf16[3,384,2048]{2,1,0:T(8,128)(2,1)}) %all-reduce.3.cloned.1.call-update) | async-done | bytes 4718608 | tf_op jit(solution)/shard_map/psum | solution.py:89
  309.6 6.5 fusion.3
  316.1 2.2 copy-done
  318.3 3.0 fusion.4
  321.3 64.5 %all-gather.9.cloned.1.call-done = bf16[2048,2,1024]{2,1,0:T(2,128)(2,1)} async-done(((bf16[128,2,1024]{2,1,0:T(2,128)(2,1)}), bf16[2048,2,1024]{2,1,0:T(2,128)(2,1)}) %all-gather.9.cloned.1.call-update) | async-done | bytes 8388624 | tf_op jit(solution)/shard_map/all_gather | solution.py:94
  385.8 10.4 %copy.27 = bf16[256,8,2,1024]{3,1,2,0:T(8,128)(2,1)} copy(bf16[256,8,2,1024]{3,2,1,0:T(2,128)(2,1)} %bitcast.97) | data formatting | bytes 16777216
  396.1 14.6 %fusion.41 = f32[1152,2048]{1,0:T(8,128)} fusion(bf16[1152,2048]{1,0:T(8,128)(2,1)S(1)} %bitcast.100, bf16[2048,2048]{1,0:T(8,128)(2,1)} %bitcast.98), kind=kOutput, calls=%fused_computation.62 | convolution fusion | flops 9663676416 | bytes 22544384 | tf_op jit(solution)/shard_map/dot_general | solution.py:97
  410.8 31.4 %all-gather.11.cloned.1.call-done = bf16[1024,2048]{1,0:T(8,128)(2,1)} async-done(((bf16[1024,128]{1,0:T(8,128)(2,1)}), bf16[1024,2048]{1,0:T(8,128)(2,1)}) %all-gather.11.cloned.1.call-update) | async-done | bytes 4194320 | tf_op jit(solution)/shard_map/all_gather | solution.py:103
  442.2 10.4 %convolution_convert_fusion = bf16[1152,2048]{1,0:T(8,128)(2,1)} fusion(bf16[1024,2048]{1,0:T(8,128)(2,1)} %all-gather.11.cloned.1.call-done, f32[1152,2048]{1,0:T(8,128)} %fusion.41), kind=kOutput, calls=%fused_computation.12 | convolution fusion | flops 4841275392 | bytes 18350080 | tf_op jit(solution)/shard_map/dot_general | solution.py:101
  452.6 199.2 %all-reduce.5.cloned.1.call-done = bf16[3,384,2048]{2,1,0:T(8,128)(2,1)} async-done(((bf16[3,384,2048]{2,1,0:T(8,128)(2,1)}), bf16[3,384,2048]{2,1,0:T(8,128)(2,1)}) %all-reduce.5.cloned.1.call-update) | async-done | bytes 4718608 | tf_op jit(solution)/shard_map/psum | solution.py:107
  651.8 8.9 %fusion.5 = bf16[3,384,2048]{2,1,0:T(8,128)(2,1)} fusion(bf16[3,384,2048]{2,1,0:T(8,128)(2,1)} %copy-done, bf16[3,384,2048]{2,1,0:T(8,128)(2,1)} %all-reduce.5.cloned.1.call-done, f32[3]{0:T(128)S(1)} %get-tuple-element.9), kind=kLoop, calls=%fused_computation.11 | loop fusion | flops 11796480 | bytes 14155788 | tf_op jit(solution)/shard_map/convert_element_type | solution.py:109
  (23 shorter events, 1.0 us)
Async XLA Ops:
  6.5 52.9 %all-gather.5.cloned.1.call-start = ((), (), s32[]{:S(2)}) async-start(), calls=%async_computation | async-start | bytes 1671168 | tf_op jit(solution)/shard_map/all_gather | solution.py:64
  7.3 96.0 %all-gather.7.cloned.1.call-start = ((), (), s32[]{:S(2)}) async-start(), calls=%async_computation.1 | async-start | bytes 1114112 | tf_op jit(solution)/shard_map/all_gather | solution.py:84
  8.0 301.6 %all-reduce.3.cloned.1.call-start = ((), (), s32[]{:S(2)}) async-start(), calls=%async_computation.2 | async-start | bytes 9437184 | tf_op jit(solution)/shard_map/psum | solution.py:89
  108.1 1.4 copy-start.2
  108.1 277.6 %all-gather.9.cloned.1.call-start = ((), (), s32[]{:S(2)}) async-start(), calls=%async_computation.3 | async-start | bytes 8912896 | tf_op jit(solution)/shard_map/all_gather | solution.py:94
  108.7 333.4 %all-gather.11.cloned.1.call-start = ((), (), s32[]{:S(2)}) async-start(), calls=%async_computation.4 | async-start | bytes 4456448 | tf_op jit(solution)/shard_map/all_gather | solution.py:103
  109.3 542.5 %all-reduce.5.cloned.1.call-start = ((), (), s32[]{:S(2)}) async-start(), calls=%async_computation.5 | async-start | bytes 9437184 | tf_op jit(solution)/shard_map/psum | solution.py:107
  316.1 2.2 copy-start
  385.8 10.4 %copy-start.1 = (bf16[3,384,2048]{2,1,0:T(8,128)(2,1)S(1)}, bf16[3,384,2048]{2,1,0:T(8,128)(2,1)}, u32[]{:S(2)}) copy-start(bf16[3,384,2048]{2,1,0:T(8,128)(2,1)} %fusion.4) | copy-start | bytes 14155780
Sparse Core Ops, SparseCore 0:
  9.8 49.6 all-gather.4
  61.7 41.4 all-gather.6
  108.3 201.3 all-reduce.2
  312.0 73.7 all-gather.8
  387.9 54.2 all-gather.10
  452.7 199.0 all-reduce.4
where the time goes:
time: 668 us
  waiting for transfers between devices  578 us (87%)
  matrix products  37.9 us (6%)
  other arithmetic  23.8 us (4%)
  local copies, waits for them, and re-layouts  14.3 us (2%)
  between operations  13.6 us (2%)
    psum x1, waiting for transfers between devices, shards(): lax.psum(attn_terms.astype(jnp.bfloat16), 'tp').astype(jnp.float32)  200 us
    psum x1, waiting for transfers between devices, shards(): mlp = lax.psum(mlp_terms.astype(jnp.bfloat16), 'tp').astype(jnp.float32)  199 us
    all_gather x1, waiting for transfers between devices, shards(): block_piece = lax.all_gather(gate_up_weight, 'var', axis=0, tiled=True)  64.5 us
    all_gather x1, waiting for transfers between devices, shards(): lax.all_gather(qkv_weight, 'var', axis=0, tiled=True)  47.8 us
    all_gather x1, waiting for transfers between devices, shards(): lax.all_gather(out_weight, 'var', axis=1, tiled=True)  32.4 us
    all_gather x1, waiting for transfers between devices, shards(): lax.all_gather(down_weight, 'var', axis=1, tiled=True)  31.4 us
    dot_general x1, matrix products, shards(): jnp.dot(columns, flat_piece, preferred_element_type=jnp.float32)  14.6 us
  transfers between devices with their start and end apart: 6, of which 6 were waited for; matrix products, arithmetic and copies ran while one was open for 7% of the time, Pallas kernels for 0%

commit v1 on v0

--- a/solution.py
+++ b/solution.py
@@ -1,3 +1,4 @@
+import functools
 import jax
 import jax.numpy as jnp
 from jax import lax
@@ -6,6 +7,22 @@
 QUERY_HEADS = 32
 KEY_VALUE_HEADS = 8
 HEAD_SIZE = 64
+
+
+def deliver_state(w_in, array_dim):
+    shaped = jnp.concatenate(
+        lax.all_to_all(
+            jnp.stack([w_in for _ in range(lax.axis_size("var"))]),
+            axis_name="var",
+            split_axis=0,
+            concat_axis=0,
+        ),
+        array_dim,
+    )
+    return shaped
+
+
+roads_keep_up = functools.partial(deliver_state, array_dim=0)
 
 
 def rms_norm(tensor):
@@ -91,7 +108,7 @@
     mlp_input = rms_norm(whole_after)
     flat_mlp = mlp_input.reshape(row_count, model_width)
     ff_local = gate_up_weight.shape[2]
-    block_piece = lax.all_gather(gate_up_weight, "var", axis=0, tiled=True)
+    block_piece = roads_keep_up(gate_up_weight)
     columns = flat_mlp
     flat_piece = block_piece.reshape(block_piece.shape[0], 2 * ff_local)
     gate_and_up = jnp.dot(columns, flat_piece, preferred_element_type=jnp.float32)

time: 668 us -> 678 us (1.015)
  local copies, waits for them, and re-layouts: 14.3 us -> 22.1 us
    psum x1, waiting for transfers between devices: 200 us -> 270 us  [shards(): lax.psum(attn_terms.astype(jnp.bfloat16), 'tp').astype(jnp.float32)]
    all_gather x1 -> x0, waiting for transfers between devices: 64.5 us -> none  [shards(): block_piece = lax.all_gather(gate_up_weight, 'var', axis=0, tiled=True)]
    all_gather x1, waiting for transfers between devices: 31.4 us -> 22.8 us  [shards(): lax.all_gather(down_weight, 'var', axis=1, tiled=True)]
    another operation x0 -> x1, local copies, waits for them, and re-layouts: none -> 7.61 us  [deliver_state(): jnp.stack([w_in for _ in range(lax.axis_size('var'))])]
  transfers between devices with their start and end apart: 6 -> 6, of which waited for: 6 -> 5; matrix products, arithmetic and copies ran while one was open for 7% -> 8% of each run, Pallas kernels for 0% -> 0%
where the time goes in v1:
time: 678 us; the launch traced here: 677 us
  waiting for transfers between devices  574 us (85%)
  matrix products  37.9 us (6%)
  other arithmetic  23.8 us (4%)
  local copies, waits for them, and re-layouts  22.1 us (3%)
  between operations  13.2 us (2%)
    psum x1, waiting for transfers between devices, shards(): lax.psum(attn_terms.astype(jnp.bfloat16), 'tp').astype(jnp.float32)  270 us
    psum x1, waiting for transfers between devices, shards(): mlp = lax.psum(mlp_terms.astype(jnp.bfloat16), 'tp').astype(jnp.float32)  199 us
    all_gather x1, waiting for transfers between devices, shards(): lax.all_gather(qkv_weight, 'var', axis=0, tiled=True)  47.8 us
    all_gather x1, waiting for transfers between devices, shards(): lax.all_gather(out_weight, 'var', axis=1, tiled=True)  32.4 us
    all_gather x1, waiting for transfers between devices, shards(): lax.all_gather(down_weight, 'var', axis=1, tiled=True)  22.8 us
    dot_general x1, matrix products, shards(): jnp.dot(columns, flat_piece, preferred_element_type=jnp.float32)  14.6 us
  transfers between devices with their start and end apart: 6, of which 5 were waited for; matrix products, arithmetic and copies ran while one was open for 8% of the time, Pallas kernels for 0%

profile of v1, /device:TPU:1, one launch (start us, length us, event | category | flops | bytes accessed | tf_op | source)
XLA Modules:
  0.0 677.2 jit_solution(10957432547419688870)
XLA Ops:
  6.5 0.7 all-gather.4.cloned.1.call-update
  7.3 0.7 all-gather.6.cloned.1.call-update
  8.1 3.3 fusion
  11.7 47.8 %all-gather.4.cloned.1.call-done = bf16[2048,384]{1,0:T(8,128)(2,1)} async-done(((bf16[128,384]{1,0:T(8,128)(2,1)}), bf16[2048,384]{1,0:T(8,128)(2,1)}) %all-gather.4.cloned.1.call-update) | async-done | bytes 1572880 | tf_op jit(solution)/shard_map/all_gather | solution.py:81
  59.5 1.7 copy.7
  61.2 4.6 fusion.9
  66.1 1.2 fusion.7
  67.3 1.5 fusion.6
  68.8 2.1 fusion.17
  70.9 32.4 %all-gather.6.cloned.1.call-done = bf16[256,2048]{1,0:T(8,128)(2,1)} async-done(((bf16[256,128]{1,0:T(8,128)(2,1)}), bf16[256,2048]{1,0:T(8,128)(2,1)}) %all-gather.6.cloned.1.call-update) | async-done | bytes 1048592 | tf_op jit(solution)/shard_map/all_gather | solution.py:101
  103.3 4.9 convolution_convert_fusion.1
  108.2 7.6 %stack.2 = bf16[16,128,2,1024]{3,2,1,0:T(2,128)(2,1)} broadcast(bf16[128,2,1024]{2,1,0:T(2,128)(2,1)S(1)} %copy-done.2), dimensions={1,2,3} | broadcast | bytes 8912896 | tf_op jit(solution)/shard_map/stack | solution.py:15
  115.8 5.9 all-to-all-start
  121.8 0.5 all-gather.8.cloned.1.call-update
  122.6 269.9 %all-reduce.3.cloned.1.call-done = bf16[3,384,2048]{2,1,0:T(8,128)(2,1)} async-done(((bf16[3,384,2048]{2,1,0:T(8,128)(2,1)}), bf16[3,384,2048]{2,1,0:T(8,128)(2,1)}) %all-reduce.3.cloned.1.call-update) | async-done | bytes 4718608 | tf_op jit(solution)/shard_map/psum | solution.py:106
  392.5 6.5 fusion.3
  399.0 2.2 copy-done
  401.1 3.0 fusion.4
  404.1 10.6 %copy.20 = bf16[256,8,2,1024]{3,1,2,0:T(8,128)(2,1)} copy(bf16[256,8,2,1024]{3,2,1,0:T(2,128)(2,1)} %bitcast.35) | data formatting | bytes 16777216
  414.7 14.6 %fusion.41 = f32[1152,2048]{1,0:T(8,128)} fusion(bf16[1152,2048]{1,0:T(8,128)(2,1)S(1)} %bitcast.100, bf16[2048,2048]{1,0:T(8,128)(2,1)} %bitcast.98), kind=kOutput, calls=%fused_computation.62 | convolution fusion | flops 9663676416 | bytes 22544384 | tf_op jit(solution)/shard_map/dot_general | solution.py:114
  429.3 22.8 %all-gather.8.cloned.1.call-done = bf16[1024,2048]{1,0:T(8,128)(2,1)} async-done(((bf16[1024,128]{1,0:T(8,128)(2,1)}), bf16[1024,2048]{1,0:T(8,128)(2,1)}) %all-gather.8.cloned.1.call-update) | async-done | bytes 4194320 | tf_op jit(solution)/shard_map/all_gather | solution.py:120
  452.1 10.4 %convolution_convert_fusion = bf16[1152,2048]{1,0:T(8,128)(2,1)} fusion(bf16[1024,2048]{1,0:T(8,128)(2,1)} %all-gather.8.cloned.1.call-done, f32[1152,2048]{1,0:T(8,128)} %fusion.41), kind=kOutput, calls=%fused_computation.12 | convolution fusion | flops 4841275392 | bytes 18350080 | tf_op jit(solution)/shard_map/dot_general | solution.py:118
  462.6 199.2 %all-reduce.5.cloned.1.call-done = bf16[3,384,2048]{2,1,0:T(8,128)(2,1)} async-done(((bf16[3,384,2048]{2,1,0:T(8,128)(2,1)}), bf16[3,384,2048]{2,1,0:T(8,128)(2,1)}) %all-reduce.5.cloned.1.call-update) | async-done | bytes 4718608 | tf_op jit(solution)/shard_map/psum | solution.py:124
  661.8 8.9 %fusion.5 = bf16[3,384,2048]{2,1,0:T(8,128)(2,1)} fusion(bf16[3,384,2048]{2,1,0:T(8,128)(2,1)} %copy-done, bf16[3,384,2048]{2,1,0:T(8,128)(2,1)} %all-reduce.5.cloned.1.call-done, f32[3]{0:T(128)S(1)} %get-tuple-element.9), kind=kLoop, calls=%fused_computation.11 | loop fusion | flops 11796480 | bytes 14155788 | tf_op jit(solution)/shard_map/convert_element_type | solution.py:126
  (25 shorter events, 1.0 us)
Async XLA Ops:
  6.5 52.9 %all-gather.4.cloned.1.call-start = ((), (), s32[]{:S(2)}) async-start(), calls=%async_computation.1 | async-start | bytes 1671168 | tf_op jit(solution)/shard_map/all_gather | solution.py:81
  7.3 96.0 %all-gather.6.cloned.1.call-start = ((), (), s32[]{:S(2)}) async-start(), calls=%async_computation.2 | async-start | bytes 1114112 | tf_op jit(solution)/shard_map/all_gather | solution.py:101
  8.0 384.5 %all-reduce.3.cloned.1.call-start = ((), (), s32[]{:S(2)}) async-start(), calls=%async_computation.3 | async-start | bytes 9437184 | tf_op jit(solution)/shard_map/psum | solution.py:106
  103.3 4.9 copy-start.2
  115.8 6.7 copy-start.3
  115.8 288.3 %all-to-all-start = ((bf16[16,128,2,1024]{3,2,1,0:T(2,128)(2,1)}), bf16[16,128,2,1024]{3,2,1,0:T(2,128)(2,1)}, u32[]{:S(2)}, u32[]{:S(2)}) async-start(bf16[16,128,2,1024]{3,2,1,0:T(2,128)(2,1)} %stack.2), calls=%async_computation | async-start | bytes 16777216 | tf_op jit(solution)/shard_map/all_to_all | solution.py:14
  121.7 330.4 %all-gather.8.cloned.1.call-start = ((), (), s32[]{:S(2)}) async-start(), calls=%async_computation.4 | async-start | bytes 4456448 | tf_op jit(solution)/shard_map/all_gather | solution.py:120
  122.3 539.5 %all-reduce.5.cloned.1.call-start = ((), (), s32[]{:S(2)}) async-start(), calls=%async_computation.5 | async-start | bytes 9437184 | tf_op jit(solution)/shard_map/psum | solution.py:124
  398.9 2.2 copy-start
  404.1 10.6 %copy-start.1 = (bf16[3,384,2048]{2,1,0:T(8,128)(2,1)S(1)}, bf16[3,384,2048]{2,1,0:T(8,128)(2,1)}, u32[]{:S(2)}) copy-start(bf16[3,384,2048]{2,1,0:T(8,128)(2,1)} %fusion.4) | copy-start | bytes 14155780
Sparse Core Ops, SparseCore 0:
  9.8 49.6 all-gather.3
  61.7 41.4 all-gather.5
  108.3 284.0 all-reduce.2
  394.6 57.5 all-gather.7
  462.7 199.0 all-reduce.4
